TPU v7x, 128 devices: a whole 4x4x4 slice. The times are simulated.
128 devices in a mesh: mem: 4 (over x_hi, core), tile: 32 (over x_lo, y, z).
Axes of the slice: x: 4 (x_hi: 2, x_lo: 2; x = x_hi * 2 + x_lo), y: 4, z: 4, core: 2. Of those that a mesh axis runs over, the one named last changes fastest.
Arguments:
- latents: float32 [24, 256], P('mem'), may hold values from -6 to 6
- basis: bfloat16 [256, 2, 512, 512], P(None, None, 'tile'), may hold values from -0.375 to 0.375
- conv_in: bfloat16 [9, 64], replicated, may hold values from -2 to 2
- conv_mid: bfloat16 [9, 64, 64], replicated, may hold values from -0.25 to 0.25
- conv_out: bfloat16 [64], replicated, may hold values from -0.75 to 0.75
- pressure_prev: float32 [2, 512, 512], P(None, 'tile'), may hold values from -6 to 6
- source: float32 [2, 512, 512], P(None, 'tile'), may hold values from -6 to 6
- perf_cells: int32 [384, 8], replicated, may hold values from 0 to 524287
- perf_count: int32 [384], replicated, may hold values from 1 to 8
- obs_perturbed: float32 [24, 384], replicated, may hold values from -6 to 6
- obs_error: float32 [384], replicated, may hold values from 0.2 to 2
Outputs:
- pressure: float32 [24, 2, 512, 512], P(None, None, 'tile', 'mem')
- well_data: float32 [24, 384], replicated
- latents_new: float32 [24, 256], P('mem')
All inputs are finite; a program needn't handle non-finite values.
Results may differ from a plain program's by a relative error of at most 0.0055.
Values may be sent and summed in bfloat16 or wider, within the bound.
A program may use at most 128 MiB of HBM per device.

v0:
```python
import math
import jax
import jax.numpy as jnp
from jax import lax
from jax.sharding import PartitionSpec as P

SWEEPS = 2
storage_coef = 1.0


def extended(cells, sides, width):
    for axis, dim in sides:
        count = lax.axis_size(axis)
        ends = count - 1
        head = lax.slice_in_dim(cells, 0, width, axis=dim)
        tail = lax.slice_in_dim(cells, cells.shape[dim] - width, cells.shape[dim], axis=dim)
        cells = jnp.concatenate(
            [
                lax.ppermute(tail, axis, [(i, (i + 1) % count) for i in range(ends)]),
                cells,
                lax.ppermute(head, axis, [((i + 1) % count, i) for i in range(ends)]),
            ],
            axis=dim,
        )
    return cells


def lift(field, conv_in):
    rows = field.shape[1] - 2
    width = field.shape[2]
    padded = jnp.pad(field, ((0, 0), (0, 0), (1, 1)))
    total = jnp.zeros((field.shape[0], conv_in.shape[1], rows, width), jnp.float32)
    for tap in range(9):
        part = padded[:, tap // 3 : tap // 3 + rows, tap % 3 : tap % 3 + width]
        total = total + conv_in[tap].astype(jnp.float32)[None, :, None, None] * part[:, None]
    return jax.nn.relu(total).astype(jnp.bfloat16)


def mix(lifted, field, conv_mid, conv_out):
    rows = field.shape[1]
    width = field.shape[2]
    padded = jnp.pad(lifted, ((0, 0), (0, 0), (0, 0), (1, 1)))
    total = jnp.zeros((field.shape[0], conv_mid.shape[1], rows, width), jnp.float32)
    for tap in range(9):
        part = padded[:, :, tap // 3 : tap // 3 + rows, tap % 3 : tap % 3 + width]
        total = total + jnp.einsum(
            "oc,zcxy->zoxy", conv_mid[tap], part, preferred_element_type=jnp.float32
        )
    deep = jax.nn.relu(total)
    return field + jnp.einsum("c,zcxy->zxy", conv_out.astype(jnp.float32), deep)


def neighbours(wide):
    zpad = jnp.pad(wide, ((0, 0), (1, 1), (0, 0), (0, 0)))
    return [
        zpad[:, 1:-1, 2:, 1:-1],
        zpad[:, 1:-1, :-2, 1:-1],
        zpad[:, 1:-1, 1:-1, 2:],
        zpad[:, 1:-1, 1:-1, :-2],
        zpad[:, 2:, 1:-1, 1:-1],
        zpad[:, :-2, 1:-1, 1:-1],
    ]


def well_terms(perm, press, perf_cells, perf_count, row_start, col_start, grid_rows, grid_cols):
    members = perm.shape[0]
    rows = perm.shape[2]
    width = perm.shape[3]
    wells = perf_cells.shape[0]
    slots = perf_cells.shape[1]
    ids = perf_cells.reshape(-1)
    layer_of = ids // (grid_rows * grid_cols)
    rest = ids % (grid_rows * grid_cols)
    row_local = rest // grid_cols - row_start
    col_local = rest % grid_cols - col_start
    inside = (row_local >= 0) & (row_local < rows) & (col_local >= 0) & (col_local < width)
    local_ids = jnp.where(inside, layer_of * rows * width + row_local * width + col_local, 0)
    used = (jnp.arange(slots)[None, :] < perf_count[:, None]).reshape(-1) & inside
    weight = used.astype(jnp.float32)
    perm_at = jnp.take(perm.reshape(members, -1), local_ids, axis=1) * weight[None, :]
    press_at = jnp.take(press.reshape(members, -1), local_ids, axis=1)
    numer = jnp.sum((perm_at * press_at).reshape(members, wells, slots), axis=2)
    weight_sum = jnp.sum(perm_at.reshape(members, wells, slots), axis=2)
    return (numer, weight_sum)


def body(
    latents,
    basis,
    conv_in,
    conv_mid,
    conv_out,
    pressure_prev,
    source,
    perf_cells,
    perf_count,
    obs_perturbed,
    obs_error,
):
    mem_dev = latents.shape[0]
    layers = basis.shape[1]
    rows = basis.shape[2]
    width = basis.shape[3]
    tile_at = lax.axis_index("tile")
    mem_at = lax.axis_index("mem")
    grid_rows = rows * lax.axis_size("tile")
    flat_basis = basis.reshape(basis.shape[0], -1)
    field = jnp.dot(latents.astype(jnp.bfloat16), flat_basis, preferred_element_type=jnp.float32)
    field = field.reshape(mem_dev, layers, rows, width)
    wide = extended(field, (("tile", 2),), 1)
    lifted = lax.map(lambda single: lift(single, conv_in), wide)
    lifted_wide = extended(lifted, (("tile", 3),), 1)
    log_perm = lax.map(lambda pair: mix(pair[0], pair[1], conv_mid, conv_out), (lifted_wide, field))
    base_full = storage_coef * pressure_prev + source
    log_tiles = lax.all_to_all(log_perm, "mem", split_axis=3, concat_axis=0, tiled=True)
    cols = log_tiles.shape[3]
    perm = jnp.exp(log_tiles)
    base = lax.dynamic_slice_in_dim(base_full, mem_at * cols, cols, 2)
    prev_local = lax.dynamic_slice_in_dim(pressure_prev, mem_at * cols, cols, 2)
    perm_wide = extended(perm, (("mem", 3), ("tile", 2)), 1)
    conduct = [2.0 * perm * other / (perm + other) for other in neighbours(perm_wide)]
    denom = storage_coef + sum(conduct)
    press = jnp.broadcast_to(prev_local, perm.shape)
    for sweep in range(SWEEPS):
        press_wide = extended(press, (("mem", 3), ("tile", 2)), 1)
        acc = base[None] + sum((cval * nval for cval, nval in zip(conduct, neighbours(press_wide))))
        press = acc / denom
    numer, weight_sum = well_terms(
        perm,
        press,
        perf_cells,
        perf_count,
        tile_at * rows,
        mem_at * cols,
        grid_rows,
        cols * lax.axis_size("mem"),
    )
    members = press.shape[0]
    numer, weight_sum = lax.psum((numer, weight_sum), ("mem", "tile"))
    well_data = numer / weight_sum
    scale = 2.0 * obs_error
    centred = well_data - jnp.mean(well_data, axis=0, keepdims=True)
    scaled = centred / (math.sqrt(members - 1) * scale[None, :])
    innov = (obs_perturbed - well_data) / scale[None, :]
    gram = jnp.eye(members, dtype=jnp.float32) + jnp.dot(
        scaled, scaled.T, precision=lax.Precision.HIGHEST
    )
    cross = jnp.dot(scaled, innov.T, precision=lax.Precision.HIGHEST)
    factor = jnp.linalg.cholesky(gram)
    weights = jax.scipy.linalg.cho_solve((factor, True), cross)
    every = lax.all_gather(latents, "mem", axis=0, tiled=True)
    spread = (every - jnp.mean(every, axis=0, keepdims=True)) / math.sqrt(members - 1)
    own_weights = lax.dynamic_slice_in_dim(weights, mem_at * mem_dev, mem_dev, 1)
    latents_new = latents + jnp.dot(own_weights.T, spread, precision=lax.Precision.HIGHEST)
    return (press, well_data, latents_new)


def solution(mesh):
    return jax.shard_map(
        body,
        mesh=mesh,
        in_specs=(
            P("mem", None),
            P(None, None, "tile", None),
            P(),
            P(),
            P(),
            P(None, "tile", None),
            P(None, "tile", None),
            P(),
            P(),
            P(),
            P(),
        ),
        out_specs=(P(None, None, "tile", "mem"), P(), P("mem", None)),
        check_vma=False,
    )
```

profile of v0, /device:TPU:1, one launch (start us, length us, event | category | flops | bytes accessed | tf_op | source)
XLA Modules:
  0.0 651.2 jit_solution(13168219996132069656)
XLA Ops:
  7.2 15.4 %copy.59 = bf16[32,8,32,512]{3,1,2,0:T(8,128)(2,1)} copy(bf16[32,8,32,512]{3,2,1,0:T(8,128)(2,1)} %bitcast.226) | data formatting | bytes 16777216
  22.6 11.9 %copy.29 = bf16[16384,256]{1,0:T(8,128)(2,1)} copy(bf16[16384,256]{0,1:T(8,128)(2,1)} %bitcast.222) | data formatting | bytes 16777216 | tf_op jit(solution)/shard_map/dot_general | solution.py:108
  34.5 5.6 fusion.110
  49.4 35.6 %while.24 = (s32[]{:T(128)}, bf16[6,2,64,16,512]{4,2,3,1,0:T(8,128)(2,1)}, bf16[9,64]{1,0:T(8,128)(2,1)S(1)}, f32[6,2,18,512]{3,0,2,1:T(8,128)S(1)}, s32[]{:T(128)}) while((s32[]{:T(128)}, bf16[6,2,64,16,512]{4,2,3,1,0:T(8,128)(2,1)}, bf16[9,64]{1,0:T(8,128)(2,1)S(1)}, f32[6,2,18,512]{3,0,2,1:T(8,128)S(1)}, s32[]{:T(128)}) %tuple.105), condition=%wide.region_1.2_spmd, body=%wide.region_0.1_spmd.sunk | while | flops 19923520 | bytes 8067265 | solution.py:111
  93.6 6.9 %collective-permute-start.7 = (f32[24,2,16,1]{3,2,1,0:T(8,128)}, f32[24,2,16,1]{3,2,1,0:T(8,128)}, u32[]{:S(2)}, u32[]{:S(2)}) collective-permute-start(f32[24,2,16,1]{3,2,1,0:T(8,128)} %broadcast_in_dim.48), channel_id=1, source_target_pairs={{0,32},{32,64},{64,96},{1,33},{33,65},{65,97},{2,34},{34,66},{66,9... | collective-permute-start | bytes 9224 | tf_op jit(solution)/shard_map/ppermute | solution.py:19
  110.0 10.3 %pad_maximum_fusion = bf16[6,2,64,18,512]{4,2,3,1,0:T(8,128)(2,1)} fusion(bf16[6,2,64,1,512]{4,2,3,1,0:T(8,128)(2,1)S(1)} %collective-permute-done.3, bf16[6,2,64,16,512]{4,2,3,1,0:T(8,128)(2,1)} %get-tuple-element.134, bf16[6,2,64,1,512]{4,2,3,1,0:T(8,128)(2,1)S(1)} %collective-permute-done.2), kind=kLoop, calls=%fused_computation.83 | loop fusion | flops 14155776 | bytes 28311552 | tf_op jit(solution)/shard_map/concatenate | solution.py:17
  120.3 224.6 %while.25 = (s32[]{:T(128)}, f32[6,2,16,512]{3,2,1,0:T(8,128)S(1)}, f32[6,2,16,512]{3,0,2,1:T(8,128)S(1)}, bf16[6,2,64,18,512]{4,2,3,1,0:T(8,128)(2,1)}, bf16[9,...) while((s32[]{:T(128)}, f32[6,2,16,512]{3,2,1,0:T(8,128)S(1)}, ...), condition=%wide.region_3.4_spmd, body=%wide.region_2.3_spmd.sunk | while | flops 1219510272 | bytes 92815952 | solution.py:113
  144.2 13.4 %fusion.170 = f32[1,2,16,512]{3,0,2,1:T(1,128)S(1)} fusion(f32[2,16,512,64]{2,3,1,0:T(8,128)} %fusion.162, f32[2,16,512,64]{2,3,1,0:T(8,128)} %fusion.163, f32[2,16,512,64]{2,3,1,0:T(8,128)} %fusion.164, f32[2,16,512,64]{2,3,1,0:T(8,128)} %fusion.165, f32[2,16,512,64]{2,3,1,0:T(8,128)} %fusion.166, f32[2,16,512,64]{2,3,1,0:T(8,128)} %fusion.167, ...), kind=kOutput, calls=%fused_computation.21.clone.1 | convolution fusion | flops 145752064 | bytes 35996160 | tf_op jit(solution)/shard_map/while/body/eval_jaxpr/c,zcxy->zxy/dot_general | solution.py:50
  181.7 13.4 %fusion.170 = f32[1,2,16,512]{3,0,2,1:T(1,128)S(1)} fusion(f32[2,16,512,64]{2,3,1,0:T(8,128)} %fusion.162, f32[2,16,512,64]{2,3,1,0:T(8,128)} %fusion.163, f32[2,16,512,64]{2,3,1,0:T(8,128)} %fusion.164, f32[2,16,512,64]{2,3,1,0:T(8,128)} %fusion.165, f32[2,16,512,64]{2,3,1,0:T(8,128)} %fusion.166, f32[2,16,512,64]{2,3,1,0:T(8,128)} %fusion.167, ...), kind=kOutput, calls=%fused_computation.21.clone.1 | convolution fusion | flops 145752064 | bytes 35996160 | tf_op jit(solution)/shard_map/while/body/eval_jaxpr/c,zcxy->zxy/dot_general | solution.py:50
  219.1 13.4 %fusion.170 = f32[1,2,16,512]{3,0,2,1:T(1,128)S(1)} fusion(f32[2,16,512,64]{2,3,1,0:T(8,128)} %fusion.162, f32[2,16,512,64]{2,3,1,0:T(8,128)} %fusion.163, f32[2,16,512,64]{2,3,1,0:T(8,128)} %fusion.164, f32[2,16,512,64]{2,3,1,0:T(8,128)} %fusion.165, f32[2,16,512,64]{2,3,1,0:T(8,128)} %fusion.166, f32[2,16,512,64]{2,3,1,0:T(8,128)} %fusion.167, ...), kind=kOutput, calls=%fused_computation.21.clone.1 | convolution fusion | flops 145752064 | bytes 35996160 | tf_op jit(solution)/shard_map/while/body/eval_jaxpr/c,zcxy->zxy/dot_general | solution.py:50
  256.6 13.4 %fusion.170 = f32[1,2,16,512]{3,0,2,1:T(1,128)S(1)} fusion(f32[2,16,512,64]{2,3,1,0:T(8,128)} %fusion.162, f32[2,16,512,64]{2,3,1,0:T(8,128)} %fusion.163, f32[2,16,512,64]{2,3,1,0:T(8,128)} %fusion.164, f32[2,16,512,64]{2,3,1,0:T(8,128)} %fusion.165, f32[2,16,512,64]{2,3,1,0:T(8,128)} %fusion.166, f32[2,16,512,64]{2,3,1,0:T(8,128)} %fusion.167, ...), kind=kOutput, calls=%fused_computation.21.clone.1 | convolution fusion | flops 145752064 | bytes 35996160 | tf_op jit(solution)/shard_map/while/body/eval_jaxpr/c,zcxy->zxy/dot_general | solution.py:50
  294.0 13.4 %fusion.170 = f32[1,2,16,512]{3,0,2,1:T(1,128)S(1)} fusion(f32[2,16,512,64]{2,3,1,0:T(8,128)} %fusion.162, f32[2,16,512,64]{2,3,1,0:T(8,128)} %fusion.163, f32[2,16,512,64]{2,3,1,0:T(8,128)} %fusion.164, f32[2,16,512,64]{2,3,1,0:T(8,128)} %fusion.165, f32[2,16,512,64]{2,3,1,0:T(8,128)} %fusion.166, f32[2,16,512,64]{2,3,1,0:T(8,128)} %fusion.167, ...), kind=kOutput, calls=%fused_computation.21.clone.1 | convolution fusion | flops 145752064 | bytes 35996160 | tf_op jit(solution)/shard_map/while/body/eval_jaxpr/c,zcxy->zxy/dot_general | solution.py:50
  331.4 13.4 %fusion.170 = f32[1,2,16,512]{3,0,2,1:T(1,128)S(1)} fusion(f32[2,16,512,64]{2,3,1,0:T(8,128)} %fusion.162, f32[2,16,512,64]{2,3,1,0:T(8,128)} %fusion.163, f32[2,16,512,64]{2,3,1,0:T(8,128)} %fusion.164, f32[2,16,512,64]{2,3,1,0:T(8,128)} %fusion.165, f32[2,16,512,64]{2,3,1,0:T(8,128)} %fusion.166, f32[2,16,512,64]{2,3,1,0:T(8,128)} %fusion.167, ...), kind=kOutput, calls=%fused_computation.21.clone.1 | convolution fusion | flops 145752064 | bytes 35996160 | tf_op jit(solution)/shard_map/while/body/eval_jaxpr/c,zcxy->zxy/dot_general | solution.py:50
  347.0 5.0 reshape.341
  352.0 7.6 %all-to-all-start = ((f32[4,1,24576]{2,1,0:T(1,128)}), f32[4,1,24576]{2,1,0:T(1,128)S(1)}, u32[]{:S(2)}, u32[]{:S(2)}) async-start(f32[4,1,24576]{2,1,0:T(1,128)} %reshape.341), calls=%async_computation | async-start | bytes 786432 | tf_op jit(solution)/shard_map/all_to_all | solution.py:115
  361.8 5.9 all-to-all-done
  404.6 4.8 fusion.71
  409.5 5.6 collective-permute-start.12
  419.8 5.9 collective-permute-done.13
  431.7 5.8 all-gather
  440.0 10.8 %gather_fusion = f32[3072,24]{1,0:T(8,128)} fusion(f32[24,4096]{0,1:T(8,128)S(1)} %copy.38, s32[3072]{0:T(1024)S(1)} %broadcast_clamp_fusion), kind=kCustom, calls=%fused_computation.clone | custom fusion | bytes 602112 | tf_op jit(solution)/shard_map/jit(_take)/gather | solution.py:80
  456.5 10.8 %gather_fusion.1 = f32[3072,24]{1,0:T(8,128)} fusion(f32[24,4096]{0,1:T(8,128)S(1)} %bitcast.225, s32[3072]{0:T(1024)S(1)} %broadcast_clamp_fusion), kind=kCustom, calls=%fused_computation.1.clone | custom fusion | bytes 602112 | tf_op jit(solution)/shard_map/jit(_take)/gather | solution.py:81
  467.4 4.6 bitcast_reduce_fusion
  472.2 161.6 %all-reduce.8.cloned.1.call-done = (f32[24,384]{0,1:T(8,128)}, f32[24,384]{0,1:T(8,128)}) async-done(((f32[24,384]{0,1:T(8,128)}, f32[24,384]{0,1:T(8,128)}), (f32[24,384]{0,1:T(8,128)}, f32[24,384]{0,1:T(8,128)})) %all-reduce.8.cloned.1.call-update) | async-done | bytes 73744 | tf_op jit(solution)/shard_map/psum | solution.py:139
  (239 shorter events, 276.3 us)
Async XLA Ops:
  40.1 5.9 collective-permute-start
  44.5 4.8 collective-permute-start.1
  85.1 18.2 %copy-start.22 = (s32[384,8]{0,1:T(8,128)S(1)}, s32[384,8]{0,1:T(8,128)}, u32[]{:S(2)}) copy-start(s32[384,8]{0,1:T(8,128)} %param.24) | copy-start | bytes 36868
  85.1 19.1 %copy-start.24 = (s32[384]{0:T(512)S(1)}, s32[384]{0:T(512)}, u32[]{:S(2)}) copy-start(s32[384]{0:T(512)} %param.25) | copy-start | bytes 4612
  87.8 18.4 %collective-permute-start.2 = (bf16[6,2,64,1,512]{4,2,3,1,0:T(8,128)(2,1)}, bf16[6,2,64,1,512]{4,2,3,1,0:T(8,128)(2,1)S(1)}, u32[]{:S(2)}, u32[]{:S(2)}) collective-permute-start(bf16[6,2,64,1,512]{4,2,3,1,0:T(8,128)(2,1)} %get-tuple-element.220), channel_id=1, source_target_pairs={{0,1},{1,2},{2,3},{3,4},{4,5},{5,6},{6,7},{7,8},{8,9},{9,10},{10,1... | collective-permute-start | bytes 2359304 | tf_op jit(solution)/shard_map/ppermute | solution.py:19
  91.2 18.8 %collective-permute-start.3 = (bf16[6,2,64,1,512]{4,2,3,1,0:T(8,128)(2,1)}, bf16[6,2,64,1,512]{4,2,3,1,0:T(8,128)(2,1)S(1)}, u32[]{:S(2)}, u32[]{:S(2)}) collective-permute-start(bf16[6,2,64,1,512]{4,2,3,1,0:T(8,128)(2,1)} %get-tuple-element.221), channel_id=1, source_target_pairs={{1,0},{2,1},{3,2},{4,3},{5,4},{6,5},{7,6},{8,7},{9,8},{10,9},{11,1... | collective-permute-start | bytes 2359304 | tf_op jit(solution)/shard_map/ppermute | solution.py:21
  93.6 292.5 %collective-permute-start.7 = (f32[24,2,16,1]{3,2,1,0:T(8,128)}, f32[24,2,16,1]{3,2,1,0:T(8,128)}, u32[]{:S(2)}, u32[]{:S(2)}) collective-permute-start(f32[24,2,16,1]{3,2,1,0:T(8,128)} %broadcast_in_dim.48), channel_id=1, source_target_pairs={{0,32},{32,64},{64,96},{1,33},{33,65},{65,97},{2,34},{34,66},{66,9... | collective-permute-start | bytes 9224 | tf_op jit(solution)/shard_map/ppermute | solution.py:19
  101.3 284.8 %collective-permute-start.8 = (f32[24,2,16,1]{3,2,1,0:T(8,128)}, f32[24,2,16,1]{3,2,1,0:T(8,128)}, u32[]{:S(2)}, u32[]{:S(2)}) collective-permute-start(f32[24,2,16,1]{3,2,1,0:T(8,128)} %broadcast_in_dim.50), channel_id=1, source_target_pairs={{32,0},{64,32},{96,64},{33,1},{65,33},{97,65},{34,2},{66,34},{98,6... | collective-permute-start | bytes 9224 | tf_op jit(solution)/shard_map/ppermute | solution.py:21
  105.0 15.3 %copy-start.20 = (bf16[64]{0:T(256)(128)(2,1)S(1)}, bf16[64]{0:T(256)(128)(2,1)}, u32[]{:S(2)}) copy-start(bf16[64]{0:T(256)(128)(2,1)} %param.21) | copy-start | bytes 388
  352.0 15.7 %all-to-all-start = ((f32[4,1,24576]{2,1,0:T(1,128)}), f32[4,1,24576]{2,1,0:T(1,128)S(1)}, u32[]{:S(2)}, u32[]{:S(2)}) async-start(f32[4,1,24576]{2,1,0:T(1,128)} %reshape.341), calls=%async_computation | async-start | bytes 786432 | tf_op jit(solution)/shard_map/all_to_all | solution.py:115
  359.6 274.3 %all-reduce.8.cloned.1.call-start = ((), (), s32[]{:S(2)}) async-start(), calls=%async_computation.1 | async-start | bytes 786432 | tf_op jit(solution)/shard_map/psum | solution.py:139
  381.4 11.5 %collective-permute-start.4 = (f32[24,2,16,1]{3,2,1,0:T(8,128)S(1)}, f32[24,2,16,1]{3,2,1,0:T(8,128)S(1)}, u32[]{:S(2)}, u32[]{:S(2)}) collective-permute-start(f32[24,2,16,1]{3,2,1,0:T(8,128)S(1)} %get-tuple-element.232), channel_id=1, source_target_pairs={{0,32},{32,64},{64,96},{1,33},{33,65},{65,97},{2,34},{34,66},{66,9... | collective-permute-start | bytes 9224 | tf_op jit(solution)/shard_map/ppermute | solution.py:19
  384.2 10.6 %collective-permute-start.5 = (f32[24,2,16,1]{3,2,1,0:T(8,128)S(1)}, f32[24,2,16,1]{3,2,1,0:T(8,128)S(1)}, u32[]{:S(2)}, u32[]{:S(2)}) collective-permute-start(f32[24,2,16,1]{3,2,1,0:T(8,128)S(1)} %get-tuple-element.233), channel_id=1, source_target_pairs={{32,0},{64,32},{96,64},{33,1},{65,33},{97,65},{34,2},{66,34},{98,6... | collective-permute-start | bytes 9224 | tf_op jit(solution)/shard_map/ppermute | solution.py:21
  387.8 12.5 %collective-permute-start.11 = (f32[24,2,1,130]{3,2,1,0:T(1,128)S(1)}, f32[24,2,1,130]{3,2,1,0:T(1,128)S(1)}, u32[]{:S(2)}, u32[]{:S(2)}) collective-permute-start(f32[24,2,1,130]{3,2,1,0:T(1,128)S(1)} %get-tuple-element.226), channel_id=1, source_target_pairs={{0,1},{1,2},{2,3},{3,4},{4,5},{5,6},{6,7},{7,8},{8,9},{9,10},{10,1... | collective-permute-start | bytes 74888 | tf_op jit(solution)/shard_map/ppermute | solution.py:19
  391.6 8.7 %collective-permute-start.9 = (f32[24,2,1,130]{3,2,1,0:T(1,128)S(1)}, f32[24,2,1,130]{3,2,1,0:T(1,128)S(1)}, u32[]{:S(2)}, u32[]{:S(2)}) collective-permute-start(f32[24,2,1,130]{3,2,1,0:T(1,128)S(1)} %get-tuple-element.227), channel_id=1, source_target_pairs={{1,0},{2,1},{3,2},{4,3},{5,4},{6,5},{7,6},{8,7},{9,8},{10,9},{11,1... | collective-permute-start | bytes 74888 | tf_op jit(solution)/shard_map/ppermute | solution.py:21
  395.2 6.9 %collective-permute-start.10 = (f32[24,2,1,130]{3,2,1,0:T(1,128)S(1)}, f32[24,2,1,130]{3,2,1,0:T(1,128)S(1)}, u32[]{:S(2)}, u32[]{:S(2)}) collective-permute-start(f32[24,2,1,130]{3,2,1,0:T(1,128)S(1)} %get-tuple-element.224), channel_id=1, source_target_pairs={{0,1},{1,2},{2,3},{3,4},{4,5},{5,6},{6,7},{7,8},{8,9},{9,10},{10,1... | collective-permute-start | bytes 74888 | tf_op jit(solution)/shard_map/ppermute | solution.py:19
  399.0 4.9 collective-permute-start.6
  409.3 22.3 %copy-start.25 = (f32[384]{0:T(512)S(1)}, f32[384]{0:T(512)}, u32[]{:S(2)}) copy-start(f32[384]{0:T(512)} %param.27) | copy-start | bytes 4612
  409.3 22.3 %copy-start.13 = (f32[6,256]{1,0:T(8,128)S(1)}, f32[6,256]{1,0:T(8,128)}, u32[]{:S(2)}) copy-start(f32[6,256]{1,0:T(8,128)} %param.17) | copy-start | bytes 18436
  409.5 10.3 %collective-permute-start.12 = (f32[24,2,16,1]{3,2,1,0:T(8,128)S(1)}, f32[24,2,16,1]{3,2,1,0:T(8,128)S(1)}, u32[]{:S(2)}, u32[]{:S(2)}) collective-permute-start(f32[24,2,16,1]{3,2,1,0:T(8,128)S(1)} %get-tuple-element.230), channel_id=1, source_target_pairs={{0,32},{32,64},{64,96},{1,33},{33,65},{65,97},{2,34},{34,66},{66,9... | collective-permute-start | bytes 9224 | tf_op jit(solution)/shard_map/ppermute | solution.py:19
  415.1 10.6 %collective-permute-start.13 = (f32[24,2,16,1]{3,2,1,0:T(8,128)S(1)}, f32[24,2,16,1]{3,2,1,0:T(8,128)S(1)}, u32[]{:S(2)}, u32[]{:S(2)}) collective-permute-start(f32[24,2,16,1]{3,2,1,0:T(8,128)S(1)} %get-tuple-element.231), channel_id=1, source_target_pairs={{32,0},{64,32},{96,64},{33,1},{65,33},{97,65},{34,2},{66,34},{98,6... | collective-permute-start | bytes 9224 | tf_op jit(solution)/shard_map/ppermute | solution.py:21
  419.8 17.7 %copy-start.4 = (f32[24,2,16,1]{3,2,1,0:T(8,128)}, f32[24,2,16,1]{3,2,1,0:T(8,128)S(1)}, u32[]{:S(2)}) copy-start(f32[24,2,16,1]{3,2,1,0:T(8,128)S(1)} %collective-permute-done.12) | copy-start | bytes 9220
  426.1 24.8 %collective-permute-start.14 = (f32[24,2,1,130]{3,2,1,0:T(1,128)S(1)}, f32[24,2,1,130]{3,2,1,0:T(1,128)S(1)}, u32[]{:S(2)}, u32[]{:S(2)}) collective-permute-start(f32[24,2,1,130]{3,2,1,0:T(1,128)S(1)} %get-tuple-element.223), channel_id=1, source_target_pairs={{1,0},{2,1},{3,2},{4,3},{5,4},{6,5},{7,6},{8,7},{9,8},{10,9},{11,1... | collective-permute-start | bytes 74888 | tf_op jit(solution)/shard_map/ppermute | solution.py:21
  427.4 23.5 %collective-permute-start.15 = (f32[24,2,1,130]{3,2,1,0:T(1,128)S(1)}, f32[24,2,1,130]{3,2,1,0:T(1,128)S(1)}, u32[]{:S(2)}, u32[]{:S(2)}) collective-permute-start(f32[24,2,1,130]{3,2,1,0:T(1,128)S(1)} %get-tuple-element.222), channel_id=1, source_target_pairs={{0,1},{1,2},{2,3},{3,4},{4,5},{5,6},{6,7},{7,8},{8,9},{9,10},{10,1... | collective-permute-start | bytes 74888 | tf_op jit(solution)/shard_map/ppermute | solution.py:19
  (20 other events, 174.6 us)
Sparse Core Ops, SparseCore 0:
  472.2 161.6 all-reduce.7
where the time goes:
time: 660 us; the launch traced here: 651 us
  matrix products  221 us (33%)
  waiting for transfers between devices  188 us (28%)
  local copies, waits for them, and re-layouts  107 us (16%)
  other arithmetic  58.8 us (9%)
  starting transfers between devices  55.2 us (8%)
  between operations  15.1 us (2%)
    psum x1, waiting for transfers between devices, body(): numer, weight_sum = lax.psum((numer, weight_sum), ('mem', 'tile'))  162 us
    dot_general x48, matrix products, mix(): jnp.einsum('oc,zcxy->zoxy', conv_mid[tap], part, preferred_element_type=j...  132 us
    dot_general x6, matrix products, mix(): return field + jnp.einsum('c,zcxy->zxy', conv_out.astype(jnp.float32), deep)  80.6 us
    ppermute x8, starting transfers between devices, extended(): lax.ppermute(tail, axis, [(i, (i + 1) % count) for i in range(ends)])  35 us
    unnamed x59, local copies, waits for them, and re-layouts  25.7 us
    convert_element_type x6, other arithmetic, lift(): return jax.nn.relu(total).astype(jnp.bfloat16)  18.8 us
    concatenate x8, other arithmetic, extended(): jnp.concatenate([lax.ppermute(tail, axis, [(i, (i + 1) % count) for i in...  17 us
    ppermute x8, waiting for transfers between devices, extended(): lax.ppermute(head, axis, [((i + 1) % count, i) for i in range(ends)])  16.6 us
  transfers between devices with their start and end apart: 18, of which 9 were waited for; matrix products, arithmetic and copies ran while one was open for 43% of the time, Pallas kernels for 0%

commit v1 on v0

--- a/solution.py
+++ b/solution.py
@@ -112,7 +112,10 @@
     lifted_wide = extended(lifted, (("tile", 3),), 1)
     log_perm = lax.map(lambda pair: mix(pair[0], pair[1], conv_mid, conv_out), (lifted_wide, field))
     base_full = storage_coef * pressure_prev + source
-    log_tiles = lax.all_to_all(log_perm, "mem", split_axis=3, concat_axis=0, tiled=True)
+    log_tiles = jnp.concatenate(
+        lax.all_to_all(jnp.stack(jnp.split(log_perm, lax.axis_size("mem"), axis=3)), "mem", 0, 0),
+        axis=0,
+    )
     cols = log_tiles.shape[3]
     perm = jnp.exp(log_tiles)
     base = lax.dynamic_slice_in_dim(base_full, mem_at * cols, cols, 2)

time: 660 us -> 634 us (0.961); the launches traced: 651 us -> 632 us
  local copies, waits for them, and re-layouts: 107 us -> 86.8 us
    unnamed x59 -> x53, local copies, waits for them, and re-layouts: 25.7 us -> 16.5 us
    exp x4 -> x3, local copies, waits for them, and re-layouts: 9.57 us -> 2.5 us  [body(): perm = jnp.exp(log_tiles)]
  transfers between devices with their start and end apart: 18 -> 18, of which waited for: 9 -> 9; matrix products, arithmetic and copies ran while one was open for 43% -> 41% of each run, Pallas kernels for 0% -> 0%
where the time goes in v1:
time: 634 us; the launch traced here: 632 us
  matrix products  221 us (35%)
  waiting for transfers between devices  190 us (30%)
  local copies, waits for them, and re-layouts  86.8 us (14%)
  other arithmetic  58.5 us (9%)
  starting transfers between devices  55.2 us (9%)
  between operations  14.6 us (2%)
    psum x1, waiting for transfers between devices, body(): numer, weight_sum = lax.psum((numer, weight_sum), ('mem', 'tile'))  162 us
    dot_general x48, matrix products, mix(): jnp.einsum('oc,zcxy->zoxy', conv_mid[tap], part, preferred_element_type=j...  132 us
    dot_general x6, matrix products, mix(): return field + jnp.einsum('c,zcxy->zxy', conv_out.astype(jnp.float32), deep)  80.6 us
    ppermute x8, starting transfers between devices, extended(): lax.ppermute(tail, axis, [(i, (i + 1) % count) for i in range(ends)])  35 us
    convert_element_type x6, other arithmetic, lift(): return jax.nn.relu(total).astype(jnp.bfloat16)  18.8 us
    concatenate x8, other arithmetic, extended(): jnp.concatenate([lax.ppermute(tail, axis, [(i, (i + 1) % count) for i in...  17 us
    unnamed x53, local copies, waits for them, and re-layouts  16.5 us
    ppermute x8, waiting for transfers between devices, extended(): lax.ppermute(head, axis, [((i + 1) % count, i) for i in range(ends)])  16.4 us
  transfers between devices with their start and end apart: 18, of which 9 were waited for; matrix products, arithmetic and copies ran while one was open for 41% of the time, Pallas kernels for 0%

profile of v1, /device:TPU:1, one launch (start us, length us, event | category | flops | bytes accessed | tf_op | source)
XLA Modules:
  0.0 632.1 jit_solution(8644126571545264271)
XLA Ops:
  7.2 15.4 %copy.55 = bf16[32,8,32,512]{3,1,2,0:T(8,128)(2,1)} copy(bf16[32,8,32,512]{3,2,1,0:T(8,128)(2,1)} %bitcast.225) | data formatting | bytes 16777216
  22.6 11.9 %copy.27 = bf16[16384,256]{1,0:T(8,128)(2,1)} copy(bf16[16384,256]{0,1:T(8,128)(2,1)} %bitcast.223) | data formatting | bytes 16777216 | tf_op jit(solution)/shard_map/dot_general | solution.py:108
  34.5 5.6 fusion.110
  40.2 4.4 collective-permute-start
  49.5 35.7 %while.24 = (s32[]{:T(128)}, bf16[6,2,64,16,512]{4,2,3,1,0:T(8,128)(2,1)}, bf16[9,64]{1,0:T(8,128)(2,1)S(1)}, f32[6,2,18,512]{3,0,2,1:T(8,128)S(1)}, s32[]{:T(128)}) while((s32[]{:T(128)}, bf16[6,2,64,16,512]{4,2,3,1,0:T(8,128)(2,1)}, bf16[9,64]{1,0:T(8,128)(2,1)S(1)}, f32[6,2,18,512]{3,0,2,1:T(8,128)S(1)}, s32[]{:T(128)}) %tuple.108), condition=%wide.region_1.2_spmd, body=%wide.region_0.1_spmd.sunk | while | flops 19923520 | bytes 8067265 | solution.py:111
  93.6 6.9 %collective-permute-start.7 = (f32[24,2,16,1]{3,2,1,0:T(8,128)}, f32[24,2,16,1]{3,2,1,0:T(8,128)}, u32[]{:S(2)}, u32[]{:S(2)}) collective-permute-start(f32[24,2,16,1]{3,2,1,0:T(8,128)} %broadcast_in_dim.48), channel_id=1, source_target_pairs={{0,32},{32,64},{64,96},{1,33},{33,65},{65,97},{2,34},{34,66},{66,9... | collective-permute-start | bytes 9224 | tf_op jit(solution)/shard_map/ppermute | solution.py:19
  110.1 10.3 %pad_maximum_fusion = bf16[6,2,64,18,512]{4,2,3,1,0:T(8,128)(2,1)} fusion(bf16[6,2,64,1,512]{4,2,3,1,0:T(8,128)(2,1)S(1)} %collective-permute-done.3, bf16[6,2,64,16,512]{4,2,3,1,0:T(8,128)(2,1)} %get-tuple-element.134, bf16[6,2,64,1,512]{4,2,3,1,0:T(8,128)(2,1)S(1)} %collective-permute-done.2), kind=kLoop, calls=%fused_computation.83 | loop fusion | flops 14155776 | bytes 28311552 | tf_op jit(solution)/shard_map/concatenate | solution.py:17
  120.4 224.8 %while.25 = (s32[]{:T(128)}, f32[6,2,16,512]{3,2,1,0:T(8,128)S(1)}, f32[6,2,16,512]{3,0,2,1:T(8,128)S(1)}, bf16[6,2,64,18,512]{4,2,3,1,0:T(8,128)(2,1)}, bf16[9,...) while((s32[]{:T(128)}, f32[6,2,16,512]{3,2,1,0:T(8,128)S(1)}, ...), condition=%wide.region_3.4_spmd, body=%wide.region_2.3_spmd.sunk | while | flops 1219510272 | bytes 92815952 | solution.py:113
  144.3 13.4 %fusion.170 = f32[1,2,16,512]{3,0,2,1:T(1,128)S(1)} fusion(f32[2,16,512,64]{2,3,1,0:T(8,128)} %fusion.162, f32[2,16,512,64]{2,3,1,0:T(8,128)} %fusion.163, f32[2,16,512,64]{2,3,1,0:T(8,128)} %fusion.164, f32[2,16,512,64]{2,3,1,0:T(8,128)} %fusion.165, f32[2,16,512,64]{2,3,1,0:T(8,128)} %fusion.166, f32[2,16,512,64]{2,3,1,0:T(8,128)} %fusion.167, ...), kind=kOutput, calls=%fused_computation.21.clone.1 | convolution fusion | flops 145752064 | bytes 35996160 | tf_op jit(solution)/shard_map/while/body/eval_jaxpr/c,zcxy->zxy/dot_general | solution.py:50
  181.8 13.4 %fusion.170 = f32[1,2,16,512]{3,0,2,1:T(1,128)S(1)} fusion(f32[2,16,512,64]{2,3,1,0:T(8,128)} %fusion.162, f32[2,16,512,64]{2,3,1,0:T(8,128)} %fusion.163, f32[2,16,512,64]{2,3,1,0:T(8,128)} %fusion.164, f32[2,16,512,64]{2,3,1,0:T(8,128)} %fusion.165, f32[2,16,512,64]{2,3,1,0:T(8,128)} %fusion.166, f32[2,16,512,64]{2,3,1,0:T(8,128)} %fusion.167, ...), kind=kOutput, calls=%fused_computation.21.clone.1 | convolution fusion | flops 145752064 | bytes 35996160 | tf_op jit(solution)/shard_map/while/body/eval_jaxpr/c,zcxy->zxy/dot_general | solution.py:50
  219.2 13.4 %fusion.170 = f32[1,2,16,512]{3,0,2,1:T(1,128)S(1)} fusion(f32[2,16,512,64]{2,3,1,0:T(8,128)} %fusion.162, f32[2,16,512,64]{2,3,1,0:T(8,128)} %fusion.163, f32[2,16,512,64]{2,3,1,0:T(8,128)} %fusion.164, f32[2,16,512,64]{2,3,1,0:T(8,128)} %fusion.165, f32[2,16,512,64]{2,3,1,0:T(8,128)} %fusion.166, f32[2,16,512,64]{2,3,1,0:T(8,128)} %fusion.167, ...), kind=kOutput, calls=%fused_computation.21.clone.1 | convolution fusion | flops 145752064 | bytes 35996160 | tf_op jit(solution)/shard_map/while/body/eval_jaxpr/c,zcxy->zxy/dot_general | solution.py:50
  256.7 13.4 %fusion.170 = f32[1,2,16,512]{3,0,2,1:T(1,128)S(1)} fusion(f32[2,16,512,64]{2,3,1,0:T(8,128)} %fusion.162, f32[2,16,512,64]{2,3,1,0:T(8,128)} %fusion.163, f32[2,16,512,64]{2,3,1,0:T(8,128)} %fusion.164, f32[2,16,512,64]{2,3,1,0:T(8,128)} %fusion.165, f32[2,16,512,64]{2,3,1,0:T(8,128)} %fusion.166, f32[2,16,512,64]{2,3,1,0:T(8,128)} %fusion.167, ...), kind=kOutput, calls=%fused_computation.21.clone.1 | convolution fusion | flops 145752064 | bytes 35996160 | tf_op jit(solution)/shard_map/while/body/eval_jaxpr/c,zcxy->zxy/dot_general | solution.py:50
  294.2 13.4 %fusion.170 = f32[1,2,16,512]{3,0,2,1:T(1,128)S(1)} fusion(f32[2,16,512,64]{2,3,1,0:T(8,128)} %fusion.162, f32[2,16,512,64]{2,3,1,0:T(8,128)} %fusion.163, f32[2,16,512,64]{2,3,1,0:T(8,128)} %fusion.164, f32[2,16,512,64]{2,3,1,0:T(8,128)} %fusion.165, f32[2,16,512,64]{2,3,1,0:T(8,128)} %fusion.166, f32[2,16,512,64]{2,3,1,0:T(8,128)} %fusion.167, ...), kind=kOutput, calls=%fused_computation.21.clone.1 | convolution fusion | flops 145752064 | bytes 35996160 | tf_op jit(solution)/shard_map/while/body/eval_jaxpr/c,zcxy->zxy/dot_general | solution.py:50
  331.6 13.4 %fusion.170 = f32[1,2,16,512]{3,0,2,1:T(1,128)S(1)} fusion(f32[2,16,512,64]{2,3,1,0:T(8,128)} %fusion.162, f32[2,16,512,64]{2,3,1,0:T(8,128)} %fusion.163, f32[2,16,512,64]{2,3,1,0:T(8,128)} %fusion.164, f32[2,16,512,64]{2,3,1,0:T(8,128)} %fusion.165, f32[2,16,512,64]{2,3,1,0:T(8,128)} %fusion.166, f32[2,16,512,64]{2,3,1,0:T(8,128)} %fusion.167, ...), kind=kOutput, calls=%fused_computation.21.clone.1 | convolution fusion | flops 145752064 | bytes 35996160 | tf_op jit(solution)/shard_map/while/body/eval_jaxpr/c,zcxy->zxy/dot_general | solution.py:50
  346.0 7.6 %all-to-all-start = ((f32[4,6,2,16,128]{4,3,2,1,0:T(8,128)}), f32[4,6,2,16,128]{4,3,2,1,0:T(8,128)S(1)}, u32[]{:S(2)}, u32[]{:S(2)}) async-start(f32[4,6,2,16,128]{4,3,2,1,0:T(8,128)} %pad_maximum_fusion.26), calls=%async_computation | async-start | bytes 786432 | tf_op jit(solution)/shard_map/all_to_all | solution.py:116
  355.0 6.7 %all-to-all-done = f32[4,6,2,16,128]{4,3,2,1,0:T(8,128)S(1)} async-done(((f32[4,6,2,16,128]{4,3,2,1,0:T(8,128)}), f32[4,6,2,16,128]{4,3,2,1,0:T(8,128)S(1)}, u32[]{:S(2)}, u32[]{:S(2)}) %all-to-all-start) | async-done | bytes 393248 | tf_op jit(solution)/shard_map/all_to_all | solution.py:116
  385.1 4.8 fusion.71
  390.0 5.6 collective-permute-start.12
  400.3 5.9 collective-permute-done.13
  412.8 5.5 all-gather
  421.4 10.8 %gather_fusion = f32[3072,24]{1,0:T(8,128)} fusion(f32[24,4096]{0,1:T(8,128)S(1)} %copy.34, s32[3072]{0:T(1024)S(1)} %broadcast_clamp_fusion), kind=kCustom, calls=%fused_computation.clone | custom fusion | bytes 602112 | tf_op jit(solution)/shard_map/jit(_take)/gather | solution.py:80
  437.9 10.8 %gather_fusion.1 = f32[3072,24]{1,0:T(8,128)} fusion(f32[24,4096]{0,1:T(8,128)S(1)} %bitcast.224, s32[3072]{0:T(1024)S(1)} %broadcast_clamp_fusion), kind=kCustom, calls=%fused_computation.1.clone | custom fusion | bytes 602112 | tf_op jit(solution)/shard_map/jit(_take)/gather | solution.py:81
  448.8 4.7 bitcast_reduce_fusion
  453.7 161.7 %all-reduce.8.cloned.1.call-done = (f32[24,384]{0,1:T(8,128)}, f32[24,384]{0,1:T(8,128)}) async-done(((f32[24,384]{0,1:T(8,128)}, f32[24,384]{0,1:T(8,128)}), (f32[24,384]{0,1:T(8,128)}, f32[24,384]{0,1:T(8,128)})) %all-reduce.8.cloned.1.call-update) | async-done | bytes 73744 | tf_op jit(solution)/shard_map/psum | solution.py:142
  (231 shorter events, 257.8 us)
Async XLA Ops:
  40.2 5.9 collective-permute-start
  44.6 4.8 collective-permute-start.1
  85.2 18.5 %copy-start.20 = (s32[384]{0:T(512)S(1)}, s32[384]{0:T(512)}, u32[]{:S(2)}) copy-start(s32[384]{0:T(512)} %param.25) | copy-start | bytes 4612
  87.9 18.4 %collective-permute-start.2 = (bf16[6,2,64,1,512]{4,2,3,1,0:T(8,128)(2,1)}, bf16[6,2,64,1,512]{4,2,3,1,0:T(8,128)(2,1)S(1)}, u32[]{:S(2)}, u32[]{:S(2)}) collective-permute-start(bf16[6,2,64,1,512]{4,2,3,1,0:T(8,128)(2,1)} %get-tuple-element.220), channel_id=1, source_target_pairs={{0,1},{1,2},{2,3},{3,4},{4,5},{5,6},{6,7},{7,8},{8,9},{9,10},{10,1... | collective-permute-start | bytes 2359304 | tf_op jit(solution)/shard_map/ppermute | solution.py:19
  91.3 18.8 %collective-permute-start.3 = (bf16[6,2,64,1,512]{4,2,3,1,0:T(8,128)(2,1)}, bf16[6,2,64,1,512]{4,2,3,1,0:T(8,128)(2,1)S(1)}, u32[]{:S(2)}, u32[]{:S(2)}) collective-permute-start(bf16[6,2,64,1,512]{4,2,3,1,0:T(8,128)(2,1)} %get-tuple-element.221), channel_id=1, source_target_pairs={{1,0},{2,1},{3,2},{4,3},{5,4},{6,5},{7,6},{8,7},{9,8},{10,9},{11,1... | collective-permute-start | bytes 2359304 | tf_op jit(solution)/shard_map/ppermute | solution.py:21
  93.6 273.0 %collective-permute-start.7 = (f32[24,2,16,1]{3,2,1,0:T(8,128)}, f32[24,2,16,1]{3,2,1,0:T(8,128)}, u32[]{:S(2)}, u32[]{:S(2)}) collective-permute-start(f32[24,2,16,1]{3,2,1,0:T(8,128)} %broadcast_in_dim.48), channel_id=1, source_target_pairs={{0,32},{32,64},{64,96},{1,33},{33,65},{65,97},{2,34},{34,66},{66,9... | collective-permute-start | bytes 9224 | tf_op jit(solution)/shard_map/ppermute | solution.py:19
  101.4 265.2 %collective-permute-start.8 = (f32[24,2,16,1]{3,2,1,0:T(8,128)}, f32[24,2,16,1]{3,2,1,0:T(8,128)}, u32[]{:S(2)}, u32[]{:S(2)}) collective-permute-start(f32[24,2,16,1]{3,2,1,0:T(8,128)} %broadcast_in_dim.50), channel_id=1, source_target_pairs={{32,0},{64,32},{96,64},{33,1},{65,33},{97,65},{34,2},{66,34},{98,6... | collective-permute-start | bytes 9224 | tf_op jit(solution)/shard_map/ppermute | solution.py:21
  346.0 15.7 %all-to-all-start = ((f32[4,6,2,16,128]{4,3,2,1,0:T(8,128)}), f32[4,6,2,16,128]{4,3,2,1,0:T(8,128)S(1)}, u32[]{:S(2)}, u32[]{:S(2)}) async-start(f32[4,6,2,16,128]{4,3,2,1,0:T(8,128)} %pad_maximum_fusion.26), calls=%async_computation | async-start | bytes 786432 | tf_op jit(solution)/shard_map/all_to_all | solution.py:116
  353.6 261.7 %all-reduce.8.cloned.1.call-start = ((), (), s32[]{:S(2)}) async-start(), calls=%async_computation.1 | async-start | bytes 786432 | tf_op jit(solution)/shard_map/psum | solution.py:142
  362.0 11.5 %collective-permute-start.4 = (f32[24,2,16,1]{3,2,1,0:T(8,128)S(1)}, f32[24,2,16,1]{3,2,1,0:T(8,128)S(1)}, u32[]{:S(2)}, u32[]{:S(2)}) collective-permute-start(f32[24,2,16,1]{3,2,1,0:T(8,128)S(1)} %get-tuple-element.232), channel_id=1, source_target_pairs={{0,32},{32,64},{64,96},{1,33},{33,65},{65,97},{2,34},{34,66},{66,9... | collective-permute-start | bytes 9224 | tf_op jit(solution)/shard_map/ppermute | solution.py:19
  364.7 10.6 %collective-permute-start.5 = (f32[24,2,16,1]{3,2,1,0:T(8,128)S(1)}, f32[24,2,16,1]{3,2,1,0:T(8,128)S(1)}, u32[]{:S(2)}, u32[]{:S(2)}) collective-permute-start(f32[24,2,16,1]{3,2,1,0:T(8,128)S(1)} %get-tuple-element.233), channel_id=1, source_target_pairs={{32,0},{64,32},{96,64},{33,1},{65,33},{97,65},{34,2},{66,34},{98,6... | collective-permute-start | bytes 9224 | tf_op jit(solution)/shard_map/ppermute | solution.py:21
  368.3 12.8 %collective-permute-start.11 = (f32[24,2,1,130]{3,2,1,0:T(1,128)S(1)}, f32[24,2,1,130]{3,2,1,0:T(1,128)S(1)}, u32[]{:S(2)}, u32[]{:S(2)}) collective-permute-start(f32[24,2,1,130]{3,2,1,0:T(1,128)S(1)} %get-tuple-element.226), channel_id=1, source_target_pairs={{0,1},{1,2},{2,3},{3,4},{4,5},{5,6},{6,7},{7,8},{8,9},{9,10},{10,1... | collective-permute-start | bytes 74888 | tf_op jit(solution)/shard_map/ppermute | solution.py:19
  372.2 8.9 %collective-permute-start.9 = (f32[24,2,1,130]{3,2,1,0:T(1,128)S(1)}, f32[24,2,1,130]{3,2,1,0:T(1,128)S(1)}, u32[]{:S(2)}, u32[]{:S(2)}) collective-permute-start(f32[24,2,1,130]{3,2,1,0:T(1,128)S(1)} %get-tuple-element.227), channel_id=1, source_target_pairs={{1,0},{2,1},{3,2},{4,3},{5,4},{6,5},{7,6},{8,7},{9,8},{10,9},{11,1... | collective-permute-start | bytes 74888 | tf_op jit(solution)/shard_map/ppermute | solution.py:21
  375.7 7.2 %collective-permute-start.10 = (f32[24,2,1,130]{3,2,1,0:T(1,128)S(1)}, f32[24,2,1,130]{3,2,1,0:T(1,128)S(1)}, u32[]{:S(2)}, u32[]{:S(2)}) collective-permute-start(f32[24,2,1,130]{3,2,1,0:T(1,128)S(1)} %get-tuple-element.224), channel_id=1, source_target_pairs={{0,1},{1,2},{2,3},{3,4},{4,5},{5,6},{6,7},{7,8},{8,9},{9,10},{10,1... | collective-permute-start | bytes 74888 | tf_op jit(solution)/shard_map/ppermute | solution.py:19
  379.6 4.8 collective-permute-start.6
  389.9 22.3 %copy-start.21 = (f32[384]{0:T(512)S(1)}, f32[384]{0:T(512)}, u32[]{:S(2)}) copy-start(f32[384]{0:T(512)} %param.27) | copy-start | bytes 4612
  389.9 22.9 %copy-start.13 = (f32[6,256]{1,0:T(8,128)S(1)}, f32[6,256]{1,0:T(8,128)}, u32[]{:S(2)}) copy-start(f32[6,256]{1,0:T(8,128)} %param.17) | copy-start | bytes 18436
  390.0 10.3 %collective-permute-start.12 = (f32[24,2,16,1]{3,2,1,0:T(8,128)S(1)}, f32[24,2,16,1]{3,2,1,0:T(8,128)S(1)}, u32[]{:S(2)}, u32[]{:S(2)}) collective-permute-start(f32[24,2,16,1]{3,2,1,0:T(8,128)S(1)} %get-tuple-element.230), channel_id=1, source_target_pairs={{0,32},{32,64},{64,96},{1,33},{33,65},{65,97},{2,34},{34,66},{66,9... | collective-permute-start | bytes 9224 | tf_op jit(solution)/shard_map/ppermute | solution.py:19
  395.6 10.6 %collective-permute-start.13 = (f32[24,2,16,1]{3,2,1,0:T(8,128)S(1)}, f32[24,2,16,1]{3,2,1,0:T(8,128)S(1)}, u32[]{:S(2)}, u32[]{:S(2)}) collective-permute-start(f32[24,2,16,1]{3,2,1,0:T(8,128)S(1)} %get-tuple-element.231), channel_id=1, source_target_pairs={{32,0},{64,32},{96,64},{33,1},{65,33},{97,65},{34,2},{66,34},{98,6... | collective-permute-start | bytes 9224 | tf_op jit(solution)/shard_map/ppermute | solution.py:21
  400.3 18.6 %copy-start.4 = (f32[24,2,16,1]{3,2,1,0:T(8,128)}, f32[24,2,16,1]{3,2,1,0:T(8,128)S(1)}, u32[]{:S(2)}) copy-start(f32[24,2,16,1]{3,2,1,0:T(8,128)S(1)} %collective-permute-done.12) | copy-start | bytes 9220
  406.6 25.6 %collective-permute-start.14 = (f32[24,2,1,130]{3,2,1,0:T(1,128)S(1)}, f32[24,2,1,130]{3,2,1,0:T(1,128)S(1)}, u32[]{:S(2)}, u32[]{:S(2)}) collective-permute-start(f32[24,2,1,130]{3,2,1,0:T(1,128)S(1)} %get-tuple-element.223), channel_id=1, source_target_pairs={{1,0},{2,1},{3,2},{4,3},{5,4},{6,5},{7,6},{8,7},{9,8},{10,9},{11,1... | collective-permute-start | bytes 74888 | tf_op jit(solution)/shard_map/ppermute | solution.py:21
  407.9 24.3 %collective-permute-start.15 = (f32[24,2,1,130]{3,2,1,0:T(1,128)S(1)}, f32[24,2,1,130]{3,2,1,0:T(1,128)S(1)}, u32[]{:S(2)}, u32[]{:S(2)}) collective-permute-start(f32[24,2,1,130]{3,2,1,0:T(1,128)S(1)} %get-tuple-element.222), channel_id=1, source_target_pairs={{0,1},{1,2},{2,3},{3,4},{4,5},{5,6},{6,7},{7,8},{8,9},{9,10},{10,1... | collective-permute-start | bytes 74888 | tf_op jit(solution)/shard_map/ppermute | solution.py:19
  448.8 168.4 %copy-start.22 = (f32[384]{0:T(512)S(1)}, f32[384]{0:T(512)}, u32[]{:S(2)}) copy-start(f32[384]{0:T(512)} %get-tuple-element.241) | copy-start | bytes 4612
  448.8 174.6 %copy-start.23 = (f32[384]{0:T(512)S(1)}, f32[384]{0:T(512)}, u32[]{:S(2)}) copy-start(f32[384]{0:T(512)} %get-tuple-element.242) | copy-start | bytes 4612
  (18 other events, 154.9 us)
Sparse Core Ops, SparseCore 0:
  453.6 161.6 all-reduce.7
